TPU v7x, 512 devices: a whole 4x4x16 slice. The times are simulated.
512 devices in a mesh: blk: 128 (over x, z_lo, y), rep: 4 (over z_hi, core).
Axes of the slice: x: 4, y: 4, z: 16 (z_hi: 2, z_lo: 8; z = z_hi * 8 + z_lo), core: 2. Of those that a mesh axis runs over, the one named last changes fastest.
Arguments:
- queries: bfloat16 [16384, 512], P('blk'), may hold values from -3.59375 to 3.59375
- keys: bfloat16 [16384, 128], P('blk'), may hold values from -6 to 6
- values: bfloat16 [16384, 128], P('blk'), may hold values from -6 to 6
- output: bfloat16 [16384, 512], P('blk'), may hold values from -6 to 6
- grad_out: bfloat16 [16384, 512], P('blk'), may hold values from -6 to 6
- lse: float32 [4, 16384], P(None, 'blk'), may hold values from -1 to 12.5
- positions: int32 [16384], P('blk'), may hold values from 0 to 1073741823, as said below
Outputs:
- grad_queries: bfloat16 [16384, 512], P('blk')
- grad_keys: bfloat16 [16384, 128], P('blk')
- grad_values: bfloat16 [16384, 128], P('blk')
Inputs may be any that keep to these rules, and one draw needn't show every extreme that they name: positions are distinct. A token's place is the number of tokens with a smaller key. Cut the places into 2 n blocks of 64 consecutive places, n = 128; the rows of each index of blk hold the places of block c in order and then those of block 2 n - 1 - c in order, with c drawn at random for each index, every c once.
All inputs are finite; a program needn't handle non-finite values.
Results may differ from a plain program's by a relative error of at most 0.005.
Values may be sent and summed in bfloat16 or wider, within the bound.
A program may use at most 64 MiB of HBM per device.

v0:
```python
import jax
import jax.numpy as jnp
from jax import lax
from jax.sharding import PartitionSpec as P


def shifted_2(shard, axis, by):
    devices = lax.axis_size(axis)
    return lax.ppermute(shard, axis, [(i, (i + by) % devices) for i in range(devices)])


def pair_terms(
    score_scale,
    query_part,
    grad_part,
    lse_part,
    delta_part,
    query_pos,
    key_part,
    value_part,
    key_pos,
):
    scores = (
        jnp.einsum("pthd,pkd->phtk", query_part, key_part, preferred_element_type=jnp.float32)
        * score_scale
    )
    visible = key_pos[:, None, None, :] <= query_pos[:, None, :, None]
    probs = jnp.where(visible, jnp.exp(scores - lse_part[:, :, :, None]), 0.0)
    probs_low = probs.astype(jnp.bfloat16)
    value_terms = jnp.einsum(
        "phtk,pthd->pkd", probs_low, grad_part, preferred_element_type=jnp.float32
    )
    grad_probs = jnp.einsum(
        "pthd,pkd->phtk", grad_part, value_part, preferred_element_type=jnp.float32
    )
    grad_scores = (probs * (grad_probs - delta_part[:, :, :, None]) * score_scale).astype(
        jnp.bfloat16
    )
    query_terms = jnp.einsum(
        "phtk,pkd->pthd", grad_scores, key_part, preferred_element_type=jnp.float32
    )
    key_terms = jnp.einsum(
        "phtk,pthd->pkd", grad_scores, query_part, preferred_element_type=jnp.float32
    )
    pair_count = query_part.shape[0]
    part_rows = query_part.shape[1]
    return (query_terms.reshape(pair_count, part_rows, -1), key_terms, value_terms)


def moved(pair, amount):
    return shifted_2((pair[0], pair[1]), "blk", amount)


def carried(pair, amount):
    return shifted_2((pair[0], pair[1]), "blk", amount)


def pick(flags, first, second):
    shape = (flags.shape[0],) + (1,) * (first.ndim - 1)
    return jnp.where(flags.reshape(shape), first, second)


def per_device(queries, keys, values, output, grad_out, lse, positions):
    cycle_size = lax.axis_size("blk")
    group_size = lax.axis_size("rep")
    cycle_pos = lax.axis_index("blk")
    group = lax.axis_index("rep")
    tok_rows = keys.shape[0]
    half_rows = tok_rows // 2
    head_dim = keys.shape[1]
    head_count = queries.shape[1] // head_dim
    score_scale = head_dim ** (-0.5)
    quarter = cycle_size // group_size
    limit = 4
    window = min(limit, quarter)
    turn_count = quarter // window
    bit_count = group_size.bit_length() - 1
    query_heads = queries.reshape(tok_rows, head_count, head_dim)
    grad_heads = grad_out.reshape(tok_rows, head_count, head_dim)
    out_heads = output.reshape(tok_rows, head_count, head_dim)
    row_delta = jnp.sum(grad_heads.astype(jnp.float32) * out_heads.astype(jnp.float32), axis=2).T
    everyone = lax.all_gather(positions, "blk", axis=0, tiled=True).reshape(cycle_size, tok_rows)
    query_lo = query_heads[:half_rows]
    query_hi = query_heads[half_rows:]
    grad_lo = grad_heads[:half_rows]
    grad_hi = grad_heads[half_rows:]
    lse_lo = lse[:, :half_rows]
    lse_hi = lse[:, half_rows:]
    delta_lo = row_delta[:, :half_rows]
    delta_hi = row_delta[:, half_rows:]
    qpos_lo = positions[:half_rows]
    qpos_hi = positions[half_rows:]
    start_pair = (keys, values)
    for place in range(bit_count):
        shifted = moved(start_pair, quarter << place)
        chosen = group >> place & 1 == 1
        start_pair = (
            jnp.where(chosen, shifted[0], start_pair[0]),
            jnp.where(chosen, shifted[1], start_pair[1]),
        )
    win_keys = start_pair[0][None]
    win_values = start_pair[1][None]
    filled = 1
    while filled < window:
        step = min(filled, window - filled)
        extra = moved((win_keys, win_values), filled)
        win_keys = jnp.concatenate([win_keys, extra[0]], axis=0)
        win_values = jnp.concatenate([win_values, extra[1]], axis=0)
        filled = filled + step
    own_terms = pair_terms(
        score_scale,
        query_lo[None],
        grad_lo[None],
        lse_lo[None],
        delta_lo[None],
        qpos_lo[None],
        keys[:half_rows][None],
        values[:half_rows][None],
        qpos_lo[None],
    )
    own_weight = jnp.where(group == 0, 1.0, 0.0).astype(jnp.float32)
    grad_keys = jnp.zeros((window, tok_rows, head_dim), jnp.float32)
    grad_values = jnp.zeros((window, tok_rows, head_dim), jnp.float32)
    grad_query = jnp.zeros((tok_rows, head_count * head_dim), jnp.float32)
    members = jnp.arange(window, dtype=jnp.int32)

    def one_turn(turn, carry):
        win_keys, win_values, grad_keys, grad_values, grad_query = carry
        owners = (cycle_pos - quarter * group - members - window * turn) % cycle_size
        owner_pos = everyone[owners]
        lower = owner_pos[:, 0] < positions[0]
        key_lo = win_keys[:, :half_rows]
        key_hi = win_keys[:, half_rows:]
        value_lo = win_values[:, :half_rows]
        value_hi = win_values[:, half_rows:]
        kpos_lo = owner_pos[:, :half_rows]
        kpos_hi = owner_pos[:, half_rows:]
        pair_shape = (window * 2,)
        query_pair = jnp.stack(
            [
                jnp.broadcast_to(query_hi, (window,) + query_hi.shape),
                pick(
                    lower,
                    jnp.broadcast_to(query_lo, (window,) + query_lo.shape),
                    jnp.broadcast_to(query_hi, (window,) + query_hi.shape),
                ),
            ],
            axis=1,
        )
        grad_pair = jnp.stack(
            [
                jnp.broadcast_to(grad_hi, (window,) + grad_hi.shape),
                pick(
                    lower,
                    jnp.broadcast_to(grad_lo, (window,) + grad_lo.shape),
                    jnp.broadcast_to(grad_hi, (window,) + grad_hi.shape),
                ),
            ],
            axis=1,
        )
        lse_pair = jnp.stack(
            [
                jnp.broadcast_to(lse_hi, (window,) + lse_hi.shape),
                pick(
                    lower,
                    jnp.broadcast_to(lse_lo, (window,) + lse_lo.shape),
                    jnp.broadcast_to(lse_hi, (window,) + lse_hi.shape),
                ),
            ],
            axis=1,
        )
        delta_pair = jnp.stack(
            [
                jnp.broadcast_to(delta_hi, (window,) + delta_hi.shape),
                pick(
                    lower,
                    jnp.broadcast_to(delta_lo, (window,) + delta_lo.shape),
                    jnp.broadcast_to(delta_hi, (window,) + delta_hi.shape),
                ),
            ],
            axis=1,
        )
        qpos_pair = jnp.stack(
            [
                jnp.broadcast_to(qpos_hi, (window, half_rows)),
                pick(
                    lower,
                    jnp.broadcast_to(qpos_lo, (window, half_rows)),
                    jnp.broadcast_to(qpos_hi, (window, half_rows)),
                ),
            ],
            axis=1,
        )
        key_pair = jnp.stack([key_lo, pick(lower, key_lo, key_hi)], axis=1)
        value_pair = jnp.stack([value_lo, pick(lower, value_lo, value_hi)], axis=1)
        kpos_pair = jnp.stack([kpos_lo, pick(lower, kpos_lo, kpos_hi)], axis=1)
        terms = pair_terms(
            score_scale,
            query_pair.reshape(pair_shape + query_pair.shape[2:]),
            grad_pair.reshape(pair_shape + grad_pair.shape[2:]),
            lse_pair.reshape(pair_shape + lse_pair.shape[2:]),
            delta_pair.reshape(pair_shape + delta_pair.shape[2:]),
            qpos_pair.reshape(pair_shape + qpos_pair.shape[2:]),
            key_pair.reshape(pair_shape + key_pair.shape[2:]),
            value_pair.reshape(pair_shape + value_pair.shape[2:]),
            kpos_pair.reshape(pair_shape + kpos_pair.shape[2:]),
        )
        query_terms = terms[0].reshape(window, 2, half_rows, head_count * head_dim)
        key_terms = terms[1].reshape(window, 2, half_rows, head_dim)
        value_terms = terms[2].reshape(window, 2, half_rows, head_dim)
        zeros_query = jnp.zeros_like(query_terms[:, 1])
        add_lo = jnp.sum(pick(lower, query_terms[:, 1], zeros_query), axis=0)
        add_hi = jnp.sum(query_terms[:, 0], axis=0) + jnp.sum(
            pick(lower, zeros_query, query_terms[:, 1]), axis=0
        )
        grad_query = grad_query + jnp.concatenate([add_lo, add_hi], axis=0)
        zeros_key = jnp.zeros_like(key_terms[:, 1])
        key_add = jnp.concatenate(
            [
                key_terms[:, 0] + pick(lower, key_terms[:, 1], zeros_key),
                pick(lower, zeros_key, key_terms[:, 1]),
            ],
            axis=1,
        )
        value_add = jnp.concatenate(
            [
                value_terms[:, 0] + pick(lower, value_terms[:, 1], zeros_key),
                pick(lower, zeros_key, value_terms[:, 1]),
            ],
            axis=1,
        )
        grad_keys = grad_keys + key_add
        grad_values = grad_values + value_add
        win_keys, win_values = shifted_2((win_keys, win_values), "blk", window)
        grad_keys, grad_values = shifted_2((grad_keys, grad_values), "blk", window)
        return (win_keys, win_values, grad_keys, grad_values, grad_query)

    final = lax.fori_loop(
        0, turn_count, one_turn, (win_keys, win_values, grad_keys, grad_values, grad_query)
    )
    grad_keys = final[2]
    grad_values = final[3]
    grad_query = final[4]
    count = window
    while count > 1:
        lead = (count + 1) // 2
        extra = carried((grad_keys[lead:count], grad_values[lead:count]), -lead)
        tail = count - lead
        grad_keys = jnp.concatenate([grad_keys[:tail] + extra[0], grad_keys[tail:lead]], axis=0)
        grad_values = jnp.concatenate(
            [grad_values[:tail] + extra[1], grad_values[tail:lead]], axis=0
        )
        count = lead
    total_keys = grad_keys[0]
    total_values = grad_values[0]
    remaining = group_size - 1 - group
    for place in range(bit_count):
        shifted = carried((total_keys, total_values), quarter << place)
        chosen = remaining >> place & 1 == 1
        total_keys = jnp.where(chosen, shifted[0], total_keys)
        total_values = jnp.where(chosen, shifted[1], total_values)
    own_pad = jnp.zeros((half_rows, head_dim), jnp.float32)
    total_keys = total_keys + own_weight * jnp.concatenate([own_terms[1][0], own_pad], axis=0)
    total_values = total_values + own_weight * jnp.concatenate([own_terms[2][0], own_pad], axis=0)
    grad_query = grad_query + own_weight * jnp.concatenate(
        [own_terms[0][0], jnp.zeros((half_rows, head_count * head_dim), jnp.float32)], axis=0
    )
    summed = lax.psum((grad_query, total_keys, total_values), "rep")
    return (
        summed[0].astype(jnp.bfloat16),
        summed[1].astype(jnp.bfloat16),
        summed[2].astype(jnp.bfloat16),
    )


def solution(mesh):
    placed = (
        P("blk", None),
        P("blk", None),
        P("blk", None),
        P("blk", None),
        P("blk", None),
        P(None, "blk"),
        P("blk"),
    )
    return jax.shard_map(
        per_device,
        mesh=mesh,
        in_specs=placed,
        out_specs=(P("blk", None), P("blk", None), P("blk", None)),
        check_vma=False,
    )
```

profile of v0, /device:TPU:4, one launch (start us, length us, event | category | flops | bytes accessed | tf_op | source)
XLA Modules:
  0.0 912.1 jit_solution(14726433039888393091)
XLA Ops:
  0.6 3.1 collective-permute-start.4
  3.7 7.7 collective-permute-start.8
  18.9 481.2 %all-gather = s32[128,1,128]{2,1,0:T(1,128)S(1)} all-gather(s32[1,1,128]{2,1,0:T(1,128)S(1)} %bitcast.269), channel_id=1, replica_groups=mesh['blk'=128,'rep'=4] {'blk'}, dimensions={0}, use_global_device_ids=true | all-gather | bytes 66048 | tf_op jit(solution)/shard_map/all_gather | solution.py:82
  500.1 42.7 %collective-permute-start.5 = (bf16[128,128]{1,0:T(8,128)(2,1)S(1)}, bf16[128,128]{1,0:T(8,128)(2,1)S(1)}, u32[]{:S(2)}, u32[]{:S(2)}) collective-permute-start(bf16[128,128]{1,0:T(8,128)(2,1)S(1)} %broadcast_select_fusion.8), channel_id=1, source_target_pairs={{0,256},{4,260},{8,264},{12,268},{16,272},{20,276},{24,280},{28,28... | collective-permute-start | bytes 98312 | tf_op jit(solution)/shard_map/ppermute | solution.py:9
  547.0 3.2 collective-permute-done.9
  552.1 8.7 collective-permute-done.6
  562.7 2.9 collective-permute-done.10
  567.5 9.3 %collective-permute-done.7 = bf16[2,128,128]{2,1,0:T(8,128)(2,1)S(1)} collective-permute-done((bf16[2,128,128]{2,1,0:T(8,128)(2,1)S(1)}, bf16[2,128,128]{2,1,0:T(8,128)(2,1)S(1)}, u32[]{:S(2)}, u32[]{:S(2)}) %collective-permute-start.7) | collective-permute-done | bytes 65568 | tf_op jit(solution)/shard_map/ppermute | solution.py:9
  577.5 4.2 collective-permute-done.11
  582.4 238.4 %while.24 = (s32[]{:T(128)}, bf16[4,128,128]{2,1,0:T(8,128)(2,1)}, bf16[4,128,128]{2,1,0:T(8,128)(2,1)}, f32[4,128,128]{2,1,0:T(8,128)S(1)}, f32[4,128,128]{2,1,...) while((s32[]{:T(128)}, bf16[4,128,128]{2,1,0:T(8,128)(2,1)}, ...), condition=%wide.region_5.6_spmd.clone, body=%wide.region_1.5_spmd.clone.sunk | while | flops 171090496 | bytes 26398304 | solution.py:238
  598.3 3.8 collective-permute-done.1
  602.1 6.8 collective-permute-done.2
  628.3 3.4 collective-permute-done.1
  631.6 7.4 collective-permute-done.2
  658.4 3.3 collective-permute-done.1
  661.7 7.5 collective-permute-done.2
  688.5 3.3 collective-permute-done.1
  691.8 7.5 collective-permute-done.2
  718.6 3.3 collective-permute-done.1
  721.9 7.5 collective-permute-done.2
  752.0 7.6 collective-permute-done.2
  775.2 4.3 collective-permute-start.3
  781.4 7.1 collective-permute-done.2
  804.1 9.8 %collective-permute-start.3 = (f32[4,128,128]{2,1,0:T(8,128)}, f32[4,128,128]{2,1,0:T(8,128)S(1)}, u32[]{:S(2)}, u32[]{:S(2)}) collective-permute-start(f32[4,128,128]{2,1,0:T(8,128)} %maximum_add_fusion.7), channel_id=1, source_target_pairs={{0,16},{4,20},{8,24},{12,28},{16,32},{20,36},{24,40},{28,44},{32,4... | collective-permute-start | bytes 786440 | tf_op jit(solution)/shard_map/while/body/eval_jaxpr/ppermute | solution.py:9
  822.9 6.8 collective-permute-start.16
  832.3 9.9 %collective-permute-start.17 = (f32[1,128,128]{2,1,0:T(8,128)S(1)}, f32[1,128,128]{2,1,0:T(8,128)S(1)}, u32[]{:S(2)}, u32[]{:S(2)}) collective-permute-start(f32[1,128,128]{2,1,0:T(8,128)S(1)} %slice.266), channel_id=1, source_target_pairs={{0,508},{4,0},{8,4},{12,8},{16,12},{20,16},{24,20},{28,24},{32,28}... | collective-permute-start | bytes 196616 | tf_op jit(solution)/shard_map/ppermute | solution.py:9
  842.2 12.8 %collective-permute-start.14 = (f32[128,128]{1,0:T(8,128)S(1)}, f32[128,128]{1,0:T(8,128)S(1)}, u32[]{:S(2)}, u32[]{:S(2)}) collective-permute-start(f32[128,128]{1,0:T(8,128)S(1)} %fusion.30), channel_id=1, source_target_pairs={{0,128},{4,132},{8,136},{12,140},{16,144},{20,148},{24,152},{28,15... | collective-permute-start | bytes 196616 | tf_op jit(solution)/shard_map/ppermute | solution.py:9
  855.0 8.4 collective-permute-start.18
  863.5 4.2 collective-permute-start.15
  867.7 3.1 collective-permute-start.19
  871.1 4.3 collective-permute-done.19
  875.4 36.7 %all-reduce.5 = (bf16[128,512]{1,0:T(8,128)(2,1)}, bf16[128,128]{1,0:T(8,128)(2,1)}, bf16[128,128]{1,0:T(8,128)(2,1)}) all-reduce(f32[128,512]{1,0:T(8,128)S(1)} %multiply_add_fusion, f32[128,128]{1,0:T(8,128)S(1)} %multiply_add_fusion.2, f32[128,128]{1,0:T(8,128)S(1)} %multiply_add_fusion.1), channel_id=1, replica_groups=mesh['blk'=128,'rep'=4] {'rep'}, use_global_device_ids=true, to_apply=%region_6.7 | all-reduce | flops 98304 | bytes 589824 | tf_op jit(solution)/shard_map/psum | solution.py:268
  (657 shorter events, 176.6 us)
Async XLA Ops:
  0.6 499.5 %collective-permute-start.4 = (bf16[128,128]{1,0:T(8,128)(2,1)}, bf16[128,128]{1,0:T(8,128)(2,1)S(1)}, u32[]{:S(2)}, u32[]{:S(2)}) collective-permute-start(bf16[128,128]{1,0:T(8,128)(2,1)} %param.10), channel_id=1, source_target_pairs={{0,128},{4,132},{8,136},{12,140},{16,144},{20,148},{24,152},{28,15... | collective-permute-start | bytes 98312 | tf_op jit(solution)/shard_map/ppermute | solution.py:9
  3.7 539.1 %collective-permute-start.8 = (bf16[128,128]{1,0:T(8,128)(2,1)}, bf16[128,128]{1,0:T(8,128)(2,1)S(1)}, u32[]{:S(2)}, u32[]{:S(2)}) collective-permute-start(bf16[128,128]{1,0:T(8,128)(2,1)} %param.11), channel_id=1, source_target_pairs={{0,128},{4,132},{8,136},{12,140},{16,144},{20,148},{24,152},{28,15... | collective-permute-start | bytes 98312 | tf_op jit(solution)/shard_map/ppermute | solution.py:9
  500.1 44.9 %collective-permute-start.5 = (bf16[128,128]{1,0:T(8,128)(2,1)S(1)}, bf16[128,128]{1,0:T(8,128)(2,1)S(1)}, u32[]{:S(2)}, u32[]{:S(2)}) collective-permute-start(bf16[128,128]{1,0:T(8,128)(2,1)S(1)} %broadcast_select_fusion.8), channel_id=1, source_target_pairs={{0,256},{4,260},{8,264},{12,268},{16,272},{20,276},{24,280},{28,28... | collective-permute-start | bytes 98312 | tf_op jit(solution)/shard_map/ppermute | solution.py:9
  545.1 15.7 %collective-permute-start.6 = (bf16[1,128,128]{2,1,0:T(8,128)(2,1)S(1)}, bf16[1,128,128]{2,1,0:T(8,128)(2,1)S(1)}, u32[]{:S(2)}, u32[]{:S(2)}) collective-permute-start(bf16[1,128,128]{2,1,0:T(8,128)(2,1)S(1)} %select_bitcast_fusion.4), channel_id=1, source_target_pairs={{0,4},{4,8},{8,12},{12,16},{16,20},{20,24},{24,28},{28,32},{32,36}... | collective-permute-start | bytes 98312 | tf_op jit(solution)/shard_map/ppermute | solution.py:9
  550.2 15.4 %collective-permute-start.10 = (bf16[1,128,128]{2,1,0:T(8,128)(2,1)S(1)}, bf16[1,128,128]{2,1,0:T(8,128)(2,1)S(1)}, u32[]{:S(2)}, u32[]{:S(2)}) collective-permute-start(bf16[1,128,128]{2,1,0:T(8,128)(2,1)S(1)} %select_bitcast_fusion.3), channel_id=1, source_target_pairs={{0,4},{4,8},{8,12},{12,16},{16,20},{20,24},{24,28},{28,32},{32,36}... | collective-permute-start | bytes 98312 | tf_op jit(solution)/shard_map/ppermute | solution.py:9
  560.8 16.1 %collective-permute-start.7 = (bf16[2,128,128]{2,1,0:T(8,128)(2,1)S(1)}, bf16[2,128,128]{2,1,0:T(8,128)(2,1)S(1)}, u32[]{:S(2)}, u32[]{:S(2)}) collective-permute-start(bf16[2,128,128]{2,1,0:T(8,128)(2,1)S(1)} %pad_maximum_fusion.8), channel_id=1, source_target_pairs={{0,8},{4,12},{8,16},{12,20},{16,24},{20,28},{24,32},{28,36},{32,40... | collective-permute-start | bytes 196616 | tf_op jit(solution)/shard_map/ppermute | solution.py:9
  565.6 16.1 %collective-permute-start.11 = (bf16[2,128,128]{2,1,0:T(8,128)(2,1)S(1)}, bf16[2,128,128]{2,1,0:T(8,128)(2,1)S(1)}, u32[]{:S(2)}, u32[]{:S(2)}) collective-permute-start(bf16[2,128,128]{2,1,0:T(8,128)(2,1)S(1)} %pad_maximum_fusion.9), channel_id=1, source_target_pairs={{0,8},{4,12},{8,16},{12,20},{16,24},{20,28},{24,32},{28,36},{32,40... | collective-permute-start | bytes 196616 | tf_op jit(solution)/shard_map/ppermute | solution.py:9
  586.2 15.9 %collective-permute-start.1 = (bf16[4,128,128]{2,1,0:T(8,128)(2,1)S(1)}, bf16[4,128,128]{2,1,0:T(8,128)(2,1)}, u32[]{:S(2)}, u32[]{:S(2)}) collective-permute-start(bf16[4,128,128]{2,1,0:T(8,128)(2,1)S(1)} %copy.100), channel_id=1, source_target_pairs={{0,16},{4,20},{8,24},{12,28},{16,32},{20,36},{24,40},{28,44},{32,4... | collective-permute-start | bytes 393224 | tf_op jit(solution)/shard_map/while/body/eval_jaxpr/ppermute | solution.py:9
  591.9 17.1 %collective-permute-start.2 = (f32[4,128,128]{2,1,0:T(8,128)S(1)}, f32[4,128,128]{2,1,0:T(8,128)S(1)}, u32[]{:S(2)}, u32[]{:S(2)}) collective-permute-start(f32[4,128,128]{2,1,0:T(8,128)S(1)} %maximum_add_fusion.6), channel_id=1, source_target_pairs={{0,16},{4,20},{8,24},{12,28},{16,32},{20,36},{24,40},{28,44},{32,4... | collective-permute-start | bytes 786440 | tf_op jit(solution)/shard_map/while/body/eval_jaxpr/ppermute | solution.py:9
  594.5 17.2 %collective-permute-start.3 = (f32[4,128,128]{2,1,0:T(8,128)}, f32[4,128,128]{2,1,0:T(8,128)S(1)}, u32[]{:S(2)}, u32[]{:S(2)}) collective-permute-start(f32[4,128,128]{2,1,0:T(8,128)} %maximum_add_fusion.7), channel_id=1, source_target_pairs={{0,16},{4,20},{8,24},{12,28},{16,32},{20,36},{24,40},{28,44},{32,4... | collective-permute-start | bytes 786440 | tf_op jit(solution)/shard_map/while/body/eval_jaxpr/ppermute | solution.py:9
  616.2 15.4 %collective-permute-start.1 = (bf16[4,128,128]{2,1,0:T(8,128)(2,1)S(1)}, bf16[4,128,128]{2,1,0:T(8,128)(2,1)}, u32[]{:S(2)}, u32[]{:S(2)}) collective-permute-start(bf16[4,128,128]{2,1,0:T(8,128)(2,1)S(1)} %copy.100), channel_id=1, source_target_pairs={{0,16},{4,20},{8,24},{12,28},{16,32},{20,36},{24,40},{28,44},{32,4... | collective-permute-start | bytes 393224 | tf_op jit(solution)/shard_map/while/body/eval_jaxpr/ppermute | solution.py:9
  621.9 17.1 %collective-permute-start.2 = (f32[4,128,128]{2,1,0:T(8,128)S(1)}, f32[4,128,128]{2,1,0:T(8,128)S(1)}, u32[]{:S(2)}, u32[]{:S(2)}) collective-permute-start(f32[4,128,128]{2,1,0:T(8,128)S(1)} %maximum_add_fusion.6), channel_id=1, source_target_pairs={{0,16},{4,20},{8,24},{12,28},{16,32},{20,36},{24,40},{28,44},{32,4... | collective-permute-start | bytes 786440 | tf_op jit(solution)/shard_map/while/body/eval_jaxpr/ppermute | solution.py:9
  624.5 17.3 %collective-permute-start.3 = (f32[4,128,128]{2,1,0:T(8,128)}, f32[4,128,128]{2,1,0:T(8,128)S(1)}, u32[]{:S(2)}, u32[]{:S(2)}) collective-permute-start(f32[4,128,128]{2,1,0:T(8,128)} %maximum_add_fusion.7), channel_id=1, source_target_pairs={{0,16},{4,20},{8,24},{12,28},{16,32},{20,36},{24,40},{28,44},{32,4... | collective-permute-start | bytes 786440 | tf_op jit(solution)/shard_map/while/body/eval_jaxpr/ppermute | solution.py:9
  646.3 15.3 %collective-permute-start.1 = (bf16[4,128,128]{2,1,0:T(8,128)(2,1)S(1)}, bf16[4,128,128]{2,1,0:T(8,128)(2,1)}, u32[]{:S(2)}, u32[]{:S(2)}) collective-permute-start(bf16[4,128,128]{2,1,0:T(8,128)(2,1)S(1)} %copy.100), channel_id=1, source_target_pairs={{0,16},{4,20},{8,24},{12,28},{16,32},{20,36},{24,40},{28,44},{32,4... | collective-permute-start | bytes 393224 | tf_op jit(solution)/shard_map/while/body/eval_jaxpr/ppermute | solution.py:9
  652.0 17.1 %collective-permute-start.2 = (f32[4,128,128]{2,1,0:T(8,128)S(1)}, f32[4,128,128]{2,1,0:T(8,128)S(1)}, u32[]{:S(2)}, u32[]{:S(2)}) collective-permute-start(f32[4,128,128]{2,1,0:T(8,128)S(1)} %maximum_add_fusion.6), channel_id=1, source_target_pairs={{0,16},{4,20},{8,24},{12,28},{16,32},{20,36},{24,40},{28,44},{32,4... | collective-permute-start | bytes 786440 | tf_op jit(solution)/shard_map/while/body/eval_jaxpr/ppermute | solution.py:9
  654.7 17.3 %collective-permute-start.3 = (f32[4,128,128]{2,1,0:T(8,128)}, f32[4,128,128]{2,1,0:T(8,128)S(1)}, u32[]{:S(2)}, u32[]{:S(2)}) collective-permute-start(f32[4,128,128]{2,1,0:T(8,128)} %maximum_add_fusion.7), channel_id=1, source_target_pairs={{0,16},{4,20},{8,24},{12,28},{16,32},{20,36},{24,40},{28,44},{32,4... | collective-permute-start | bytes 786440 | tf_op jit(solution)/shard_map/while/body/eval_jaxpr/ppermute | solution.py:9
  682.1 17.1 %collective-permute-start.2 = (f32[4,128,128]{2,1,0:T(8,128)S(1)}, f32[4,128,128]{2,1,0:T(8,128)S(1)}, u32[]{:S(2)}, u32[]{:S(2)}) collective-permute-start(f32[4,128,128]{2,1,0:T(8,128)S(1)} %maximum_add_fusion.6), channel_id=1, source_target_pairs={{0,16},{4,20},{8,24},{12,28},{16,32},{20,36},{24,40},{28,44},{32,4... | collective-permute-start | bytes 786440 | tf_op jit(solution)/shard_map/while/body/eval_jaxpr/ppermute | solution.py:9
  684.8 17.3 %collective-permute-start.3 = (f32[4,128,128]{2,1,0:T(8,128)}, f32[4,128,128]{2,1,0:T(8,128)S(1)}, u32[]{:S(2)}, u32[]{:S(2)}) collective-permute-start(f32[4,128,128]{2,1,0:T(8,128)} %maximum_add_fusion.7), channel_id=1, source_target_pairs={{0,16},{4,20},{8,24},{12,28},{16,32},{20,36},{24,40},{28,44},{32,4... | collective-permute-start | bytes 786440 | tf_op jit(solution)/shard_map/while/body/eval_jaxpr/ppermute | solution.py:9
  712.2 17.1 %collective-permute-start.2 = (f32[4,128,128]{2,1,0:T(8,128)S(1)}, f32[4,128,128]{2,1,0:T(8,128)S(1)}, u32[]{:S(2)}, u32[]{:S(2)}) collective-permute-start(f32[4,128,128]{2,1,0:T(8,128)S(1)} %maximum_add_fusion.6), channel_id=1, source_target_pairs={{0,16},{4,20},{8,24},{12,28},{16,32},{20,36},{24,40},{28,44},{32,4... | collective-permute-start | bytes 786440 | tf_op jit(solution)/shard_map/while/body/eval_jaxpr/ppermute | solution.py:9
  714.9 17.3 %collective-permute-start.3 = (f32[4,128,128]{2,1,0:T(8,128)}, f32[4,128,128]{2,1,0:T(8,128)S(1)}, u32[]{:S(2)}, u32[]{:S(2)}) collective-permute-start(f32[4,128,128]{2,1,0:T(8,128)} %maximum_add_fusion.7), channel_id=1, source_target_pairs={{0,16},{4,20},{8,24},{12,28},{16,32},{20,36},{24,40},{28,44},{32,4... | collective-permute-start | bytes 786440 | tf_op jit(solution)/shard_map/while/body/eval_jaxpr/ppermute | solution.py:9
  733.8 15.8 %collective-permute-start = (bf16[4,128,128]{2,1,0:T(8,128)(2,1)S(1)}, bf16[4,128,128]{2,1,0:T(8,128)(2,1)}, u32[]{:S(2)}, u32[]{:S(2)}) collective-permute-start(bf16[4,128,128]{2,1,0:T(8,128)(2,1)S(1)} %copy.99), channel_id=1, source_target_pairs={{0,16},{4,20},{8,24},{12,28},{16,32},{20,36},{24,40},{28,44},{32,4... | collective-permute-start | bytes 393224 | tf_op jit(solution)/shard_map/while/body/eval_jaxpr/ppermute | solution.py:9
  742.3 17.3 %collective-permute-start.2 = (f32[4,128,128]{2,1,0:T(8,128)S(1)}, f32[4,128,128]{2,1,0:T(8,128)S(1)}, u32[]{:S(2)}, u32[]{:S(2)}) collective-permute-start(f32[4,128,128]{2,1,0:T(8,128)S(1)} %maximum_add_fusion.6), channel_id=1, source_target_pairs={{0,16},{4,20},{8,24},{12,28},{16,32},{20,36},{24,40},{28,44},{32,4... | collective-permute-start | bytes 786440 | tf_op jit(solution)/shard_map/while/body/eval_jaxpr/ppermute | solution.py:9
  745.0 17.4 %collective-permute-start.3 = (f32[4,128,128]{2,1,0:T(8,128)}, f32[4,128,128]{2,1,0:T(8,128)S(1)}, u32[]{:S(2)}, u32[]{:S(2)}) collective-permute-start(f32[4,128,128]{2,1,0:T(8,128)} %maximum_add_fusion.7), channel_id=1, source_target_pairs={{0,16},{4,20},{8,24},{12,28},{16,32},{20,36},{24,40},{28,44},{32,4... | collective-permute-start | bytes 786440 | tf_op jit(solution)/shard_map/while/body/eval_jaxpr/ppermute | solution.py:9
  764.1 17.2 %collective-permute-start = (bf16[4,128,128]{2,1,0:T(8,128)(2,1)S(1)}, bf16[4,128,128]{2,1,0:T(8,128)(2,1)}, u32[]{:S(2)}, u32[]{:S(2)}) collective-permute-start(bf16[4,128,128]{2,1,0:T(8,128)(2,1)S(1)} %copy.99), channel_id=1, source_target_pairs={{0,16},{4,20},{8,24},{12,28},{16,32},{20,36},{24,40},{28,44},{32,4... | collective-permute-start | bytes 393224 | tf_op jit(solution)/shard_map/while/body/eval_jaxpr/ppermute | solution.py:9
  772.6 15.9 %collective-permute-start.2 = (f32[4,128,128]{2,1,0:T(8,128)S(1)}, f32[4,128,128]{2,1,0:T(8,128)S(1)}, u32[]{:S(2)}, u32[]{:S(2)}) collective-permute-start(f32[4,128,128]{2,1,0:T(8,128)S(1)} %maximum_add_fusion.6), channel_id=1, source_target_pairs={{0,16},{4,20},{8,24},{12,28},{16,32},{20,36},{24,40},{28,44},{32,4... | collective-permute-start | bytes 786440 | tf_op jit(solution)/shard_map/while/body/eval_jaxpr/ppermute | solution.py:9
  775.2 16.0 %collective-permute-start.3 = (f32[4,128,128]{2,1,0:T(8,128)}, f32[4,128,128]{2,1,0:T(8,128)S(1)}, u32[]{:S(2)}, u32[]{:S(2)}) collective-permute-start(f32[4,128,128]{2,1,0:T(8,128)} %maximum_add_fusion.7), channel_id=1, source_target_pairs={{0,16},{4,20},{8,24},{12,28},{16,32},{20,36},{24,40},{28,44},{32,4... | collective-permute-start | bytes 786440 | tf_op jit(solution)/shard_map/while/body/eval_jaxpr/ppermute | solution.py:9
  792.9 22.7 %collective-permute-start = (bf16[4,128,128]{2,1,0:T(8,128)(2,1)S(1)}, bf16[4,128,128]{2,1,0:T(8,128)(2,1)}, u32[]{:S(2)}, u32[]{:S(2)}) collective-permute-start(bf16[4,128,128]{2,1,0:T(8,128)(2,1)S(1)} %copy.99), channel_id=1, source_target_pairs={{0,16},{4,20},{8,24},{12,28},{16,32},{20,36},{24,40},{28,44},{32,4... | collective-permute-start | bytes 393224 | tf_op jit(solution)/shard_map/while/body/eval_jaxpr/ppermute | solution.py:9
  795.7 19.9 %collective-permute-start.1 = (bf16[4,128,128]{2,1,0:T(8,128)(2,1)S(1)}, bf16[4,128,128]{2,1,0:T(8,128)(2,1)}, u32[]{:S(2)}, u32[]{:S(2)}) collective-permute-start(bf16[4,128,128]{2,1,0:T(8,128)(2,1)S(1)} %copy.100), channel_id=1, source_target_pairs={{0,16},{4,20},{8,24},{12,28},{16,32},{20,36},{24,40},{28,44},{32,4... | collective-permute-start | bytes 393224 | tf_op jit(solution)/shard_map/while/body/eval_jaxpr/ppermute | solution.py:9
  801.4 15.8 %collective-permute-start.2 = (f32[4,128,128]{2,1,0:T(8,128)S(1)}, f32[4,128,128]{2,1,0:T(8,128)S(1)}, u32[]{:S(2)}, u32[]{:S(2)}) collective-permute-start(f32[4,128,128]{2,1,0:T(8,128)S(1)} %maximum_add_fusion.6), channel_id=1, source_target_pairs={{0,16},{4,20},{8,24},{12,28},{16,32},{20,36},{24,40},{28,44},{32,4... | collective-permute-start | bytes 786440 | tf_op jit(solution)/shard_map/while/body/eval_jaxpr/ppermute | solution.py:9
  804.1 16.0 %collective-permute-start.3 = (f32[4,128,128]{2,1,0:T(8,128)}, f32[4,128,128]{2,1,0:T(8,128)S(1)}, u32[]{:S(2)}, u32[]{:S(2)}) collective-permute-start(f32[4,128,128]{2,1,0:T(8,128)} %maximum_add_fusion.7), channel_id=1, source_target_pairs={{0,16},{4,20},{8,24},{12,28},{16,32},{20,36},{24,40},{28,44},{32,4... | collective-permute-start | bytes 786440 | tf_op jit(solution)/shard_map/while/body/eval_jaxpr/ppermute | solution.py:9
  832.3 22.7 %collective-permute-start.17 = (f32[1,128,128]{2,1,0:T(8,128)S(1)}, f32[1,128,128]{2,1,0:T(8,128)S(1)}, u32[]{:S(2)}, u32[]{:S(2)}) collective-permute-start(f32[1,128,128]{2,1,0:T(8,128)S(1)} %slice.266), channel_id=1, source_target_pairs={{0,508},{4,0},{8,4},{12,8},{16,12},{20,16},{24,20},{28,24},{32,28}... | collective-permute-start | bytes 196616 | tf_op jit(solution)/shard_map/ppermute | solution.py:9
  842.2 21.2 %collective-permute-start.14 = (f32[128,128]{1,0:T(8,128)S(1)}, f32[128,128]{1,0:T(8,128)S(1)}, u32[]{:S(2)}, u32[]{:S(2)}) collective-permute-start(f32[128,128]{1,0:T(8,128)S(1)} %fusion.30), channel_id=1, source_target_pairs={{0,128},{4,132},{8,136},{12,140},{16,144},{20,148},{24,152},{28,15... | collective-permute-start | bytes 196616 | tf_op jit(solution)/shard_map/ppermute | solution.py:9
  (129 other events, 858.1 us)
where the time goes:
time: 914 us; the launch traced here: 912 us
  blocking collectives  518 us (57%)
  starting transfers between devices  185 us (20%)
  waiting for transfers between devices  128 us (14%)
  local copies, waits for them, and re-layouts  39.5 us (4%)
  matrix products  19.5 us (2%)
  other arithmetic  18.2 us (2%)
    all_gather x1, blocking collectives, per_device(): lax.all_gather(positions, 'blk', axis=0, tiled=True)  481 us
    ppermute x48, starting transfers between devices, shifted_2(): lax.ppermute(shard, axis, [(i, (i + by) % devices) for i in range(devices)])  185 us
    ppermute x48, waiting for transfers between devices, shifted_2(): lax.ppermute(shard, axis, [(i, (i + by) % devices) for i in range(devices)])  128 us
    psum x1, blocking collectives, per_device(): summed = lax.psum((grad_query, total_keys, total_values), 'rep')  36.7 us
    while x224, local copies, waits for them, and re-layouts  20.4 us
  transfers between devices with their start and end apart: 48, of which 31 were waited for; matrix products, arithmetic and copies ran while one was open for 7% of the time, Pallas kernels for 0%

commit v1 on v0

--- a/solution.py
+++ b/solution.py
@@ -79,7 +79,9 @@
     grad_heads = grad_out.reshape(tok_rows, head_count, head_dim)
     out_heads = output.reshape(tok_rows, head_count, head_dim)
     row_delta = jnp.sum(grad_heads.astype(jnp.float32) * out_heads.astype(jnp.float32), axis=2).T
-    everyone = lax.all_gather(positions, "blk", axis=0, tiled=True).reshape(cycle_size, tok_rows)
+    everyone = jnp.concatenate(
+        lax.all_to_all(jnp.stack([positions] * lax.axis_size("blk")), "blk", 0, 0), axis=0
+    ).reshape(cycle_size, tok_rows)
     query_lo = query_heads[:half_rows]
     query_hi = query_heads[half_rows:]
     grad_lo = grad_heads[:half_rows]

time: 914 us -> 412 us (0.45)
  the two profiles are of different devices: /device:TPU:4 before, /device:TPU:8 now
where the time goes in v1:
time: 412 us; the launch traced here: 410 us
  starting transfers between devices  145 us (35%)
  waiting for transfers between devices  140 us (34%)
  blocking collectives  43.2 us (10%)
  local copies, waits for them, and re-layouts  39.5 us (10%)
  matrix products  19.5 us (5%)
  other arithmetic  18.1 us (4%)
    ppermute x48, waiting for transfers between devices, shifted_2(): lax.ppermute(shard, axis, [(i, (i + by) % devices) for i in range(devices)])  140 us
    ppermute x48, starting transfers between devices, shifted_2(): lax.ppermute(shard, axis, [(i, (i + by) % devices) for i in range(devices)])  127 us
    psum x1, blocking collectives, per_device(): summed = lax.psum((grad_query, total_keys, total_values), 'rep')  43.2 us
    while x224, local copies, waits for them, and re-layouts  20.2 us
    all_to_all x1, starting transfers between devices, per_device(): lax.all_to_all(jnp.stack([positions] * lax.axis_size('blk')), 'blk', 0, 0)  18.3 us
  transfers between devices with their start and end apart: 49, of which 40 were waited for; matrix products, arithmetic and copies ran while one was open for 15% of the time, Pallas kernels for 0%

profile of v1, /device:TPU:8, one launch (start us, length us, event | category | flops | bytes accessed | tf_op | source)
XLA Modules:
  0.0 409.9 jit_solution(14919865831735459916)
XLA Ops:
  0.6 3.5 collective-permute-start.4
  4.2 3.4 collective-permute-start.8
  8.9 18.3 %all-to-all-start = ((s32[128,1,128]{2,1,0:T(1,128)}), s32[128,1,128]{2,1,0:T(1,128)S(1)}, u32[]{:S(2)}, u32[]{:S(2)}) async-start(s32[128,1,128]{2,1,0:T(1,128)} %stack.138), calls=%async_computation | async-start | bytes 131072 | tf_op jit(solution)/shard_map/all_to_all | solution.py:83
  33.5 5.2 %collective-permute-start.5 = (bf16[128,128]{1,0:T(8,128)(2,1)S(1)}, bf16[128,128]{1,0:T(8,128)(2,1)S(1)}, u32[]{:S(2)}, u32[]{:S(2)}) collective-permute-start(bf16[128,128]{1,0:T(8,128)(2,1)S(1)} %broadcast_select_fusion.8), channel_id=1, source_target_pairs={{0,256},{4,260},{8,264},{12,268},{16,272},{20,276},{24,280},{28,28... | collective-permute-start | bytes 98312 | tf_op jit(solution)/shard_map/ppermute | solution.py:9
  40.9 3.4 collective-permute-start.6
  46.1 3.4 collective-permute-start.10
  49.5 4.0 collective-permute-start.7
  53.5 4.3 %collective-permute-start.11 = (bf16[2,128,128]{2,1,0:T(8,128)(2,1)S(1)}, bf16[2,128,128]{2,1,0:T(8,128)(2,1)S(1)}, u32[]{:S(2)}, u32[]{:S(2)}) collective-permute-start(bf16[2,128,128]{2,1,0:T(8,128)(2,1)S(1)} %pad_maximum_fusion.9), channel_id=1, source_target_pairs={{0,8},{4,12},{8,16},{12,20},{16,24},{20,28},{24,32},{28,36},{32,40... | collective-permute-start | bytes 196616 | tf_op jit(solution)/shard_map/ppermute | solution.py:9
  57.8 9.4 %collective-permute-done.7 = bf16[2,128,128]{2,1,0:T(8,128)(2,1)S(1)} collective-permute-done((bf16[2,128,128]{2,1,0:T(8,128)(2,1)S(1)}, bf16[2,128,128]{2,1,0:T(8,128)(2,1)S(1)}, u32[]{:S(2)}, u32[]{:S(2)}) %collective-permute-start.7) | collective-permute-done | bytes 65568 | tf_op jit(solution)/shard_map/ppermute | solution.py:9
  71.5 250.6 %while.24 = (s32[]{:T(128)}, bf16[4,128,128]{2,1,0:T(8,128)(2,1)}, bf16[4,128,128]{2,1,0:T(8,128)(2,1)}, f32[4,128,128]{2,1,0:T(8,128)S(1)}, f32[4,128,128]{2,1,...) while((s32[]{:T(128)}, bf16[4,128,128]{2,1,0:T(8,128)(2,1)}, ...), condition=%wide.region_5.6_spmd.clone, body=%wide.region_1.5_spmd.clone.sunk | while | flops 171090496 | bytes 26398304 | solution.py:240
  88.2 3.2 collective-permute-done.1
  91.4 7.9 %collective-permute-done.2 = f32[4,128,128]{2,1,0:T(8,128)S(1)} collective-permute-done((f32[4,128,128]{2,1,0:T(8,128)S(1)}, f32[4,128,128]{2,1,0:T(8,128)S(1)}, u32[]{:S(2)}, u32[]{:S(2)}) %collective-permute-start.2) | collective-permute-done | bytes 262176 | tf_op jit(solution)/shard_map/while/body/eval_jaxpr/ppermute | solution.py:9
  119.5 3.7 collective-permute-done.1
  123.1 7.5 %collective-permute-done.2 = f32[4,128,128]{2,1,0:T(8,128)S(1)} collective-permute-done((f32[4,128,128]{2,1,0:T(8,128)S(1)}, f32[4,128,128]{2,1,0:T(8,128)S(1)}, u32[]{:S(2)}, u32[]{:S(2)}) %collective-permute-start.2) | collective-permute-done | bytes 262176 | tf_op jit(solution)/shard_map/while/body/eval_jaxpr/ppermute | solution.py:9
  150.8 3.7 collective-permute-done.1
  154.4 7.5 %collective-permute-done.2 = f32[4,128,128]{2,1,0:T(8,128)S(1)} collective-permute-done((f32[4,128,128]{2,1,0:T(8,128)S(1)}, f32[4,128,128]{2,1,0:T(8,128)S(1)}, u32[]{:S(2)}, u32[]{:S(2)}) %collective-permute-start.2) | collective-permute-done | bytes 262176 | tf_op jit(solution)/shard_map/while/body/eval_jaxpr/ppermute | solution.py:9
  182.1 3.7 collective-permute-done.1
  185.7 7.5 %collective-permute-done.2 = f32[4,128,128]{2,1,0:T(8,128)S(1)} collective-permute-done((f32[4,128,128]{2,1,0:T(8,128)S(1)}, f32[4,128,128]{2,1,0:T(8,128)S(1)}, u32[]{:S(2)}, u32[]{:S(2)}) %collective-permute-start.2) | collective-permute-done | bytes 262176 | tf_op jit(solution)/shard_map/while/body/eval_jaxpr/ppermute | solution.py:9
  213.4 3.7 collective-permute-done.1
  217.0 7.5 %collective-permute-done.2 = f32[4,128,128]{2,1,0:T(8,128)S(1)} collective-permute-done((f32[4,128,128]{2,1,0:T(8,128)S(1)}, f32[4,128,128]{2,1,0:T(8,128)S(1)}, u32[]{:S(2)}, u32[]{:S(2)}) %collective-permute-start.2) | collective-permute-done | bytes 262176 | tf_op jit(solution)/shard_map/while/body/eval_jaxpr/ppermute | solution.py:9
  244.7 3.7 collective-permute-done.1
  248.3 7.5 %collective-permute-done.2 = f32[4,128,128]{2,1,0:T(8,128)S(1)} collective-permute-done((f32[4,128,128]{2,1,0:T(8,128)S(1)}, f32[4,128,128]{2,1,0:T(8,128)S(1)}, u32[]{:S(2)}, u32[]{:S(2)}) %collective-permute-start.2) | collective-permute-done | bytes 262176 | tf_op jit(solution)/shard_map/while/body/eval_jaxpr/ppermute | solution.py:9
  276.0 3.7 collective-permute-done.1
  279.6 7.5 %collective-permute-done.2 = f32[4,128,128]{2,1,0:T(8,128)S(1)} collective-permute-done((f32[4,128,128]{2,1,0:T(8,128)S(1)}, f32[4,128,128]{2,1,0:T(8,128)S(1)}, u32[]{:S(2)}, u32[]{:S(2)}) %collective-permute-start.2) | collective-permute-done | bytes 262176 | tf_op jit(solution)/shard_map/while/body/eval_jaxpr/ppermute | solution.py:9
  307.3 3.8 collective-permute-done.1
  311.0 7.5 %collective-permute-done.2 = f32[4,128,128]{2,1,0:T(8,128)S(1)} collective-permute-done((f32[4,128,128]{2,1,0:T(8,128)S(1)}, f32[4,128,128]{2,1,0:T(8,128)S(1)}, u32[]{:S(2)}, u32[]{:S(2)}) %collective-permute-start.2) | collective-permute-done | bytes 262176 | tf_op jit(solution)/shard_map/while/body/eval_jaxpr/ppermute | solution.py:9
  324.2 9.5 %collective-permute-start.16 = (f32[2,128,128]{2,1,0:T(8,128)S(1)}, f32[2,128,128]{2,1,0:T(8,128)S(1)}, u32[]{:S(2)}, u32[]{:S(2)}) collective-permute-start(f32[2,128,128]{2,1,0:T(8,128)S(1)} %slice.236), channel_id=1, source_target_pairs={{0,504},{4,508},{8,0},{12,4},{16,8},{20,12},{24,16},{28,20},{32,24... | collective-permute-start | bytes 393224 | tf_op jit(solution)/shard_map/ppermute | solution.py:9
  333.8 11.7 %collective-permute-start.13 = (f32[1,128,128]{2,1,0:T(8,128)S(1)}, f32[1,128,128]{2,1,0:T(8,128)S(1)}, u32[]{:S(2)}, u32[]{:S(2)}) collective-permute-start(f32[1,128,128]{2,1,0:T(8,128)S(1)} %slice.264), channel_id=1, source_target_pairs={{0,508},{4,0},{8,4},{12,8},{16,12},{20,16},{24,20},{28,24},{32,28}... | collective-permute-start | bytes 196616 | tf_op jit(solution)/shard_map/ppermute | solution.py:9
  355.4 3.1 collective-permute-start.15
  359.1 3.7 collective-permute-start.19
  363.1 3.7 collective-permute-done.19
  366.8 43.2 %all-reduce.5 = (bf16[128,512]{1,0:T(8,128)(2,1)}, bf16[128,128]{1,0:T(8,128)(2,1)}, bf16[128,128]{1,0:T(8,128)(2,1)}) all-reduce(f32[128,512]{1,0:T(8,128)S(1)} %multiply_add_fusion, f32[128,128]{1,0:T(8,128)S(1)} %multiply_add_fusion.2, f32[128,128]{1,0:T(8,128)S(1)} %multiply_add_fusion.1), channel_id=1, replica_groups=mesh['blk'=128,'rep'=4] {'rep'}, use_global_device_ids=true, to_apply=%region_6.7 | all-reduce | flops 98304 | bytes 589824 | tf_op jit(solution)/shard_map/psum | solution.py:270
  (661 shorter events, 186.8 us)
Async XLA Ops:
  0.6 32.8 %collective-permute-start.4 = (bf16[128,128]{1,0:T(8,128)(2,1)}, bf16[128,128]{1,0:T(8,128)(2,1)S(1)}, u32[]{:S(2)}, u32[]{:S(2)}) collective-permute-start(bf16[128,128]{1,0:T(8,128)(2,1)} %param.10), channel_id=1, source_target_pairs={{0,128},{4,132},{8,136},{12,140},{16,144},{20,148},{24,152},{28,15... | collective-permute-start | bytes 98312 | tf_op jit(solution)/shard_map/ppermute | solution.py:9
  4.2 34.5 %collective-permute-start.8 = (bf16[128,128]{1,0:T(8,128)(2,1)}, bf16[128,128]{1,0:T(8,128)(2,1)S(1)}, u32[]{:S(2)}, u32[]{:S(2)}) collective-permute-start(bf16[128,128]{1,0:T(8,128)(2,1)} %param.11), channel_id=1, source_target_pairs={{0,128},{4,132},{8,136},{12,140},{16,144},{20,148},{24,152},{28,15... | collective-permute-start | bytes 98312 | tf_op jit(solution)/shard_map/ppermute | solution.py:9
  8.9 62.5 %all-to-all-start = ((s32[128,1,128]{2,1,0:T(1,128)}), s32[128,1,128]{2,1,0:T(1,128)S(1)}, u32[]{:S(2)}, u32[]{:S(2)}) async-start(s32[128,1,128]{2,1,0:T(1,128)} %stack.138), calls=%async_computation | async-start | bytes 131072 | tf_op jit(solution)/shard_map/all_to_all | solution.py:83
  49.5 17.8 %collective-permute-start.7 = (bf16[2,128,128]{2,1,0:T(8,128)(2,1)S(1)}, bf16[2,128,128]{2,1,0:T(8,128)(2,1)S(1)}, u32[]{:S(2)}, u32[]{:S(2)}) collective-permute-start(bf16[2,128,128]{2,1,0:T(8,128)(2,1)S(1)} %pad_maximum_fusion.8), channel_id=1, source_target_pairs={{0,8},{4,12},{8,16},{12,20},{16,24},{20,28},{24,32},{28,36},{32,40... | collective-permute-start | bytes 196616 | tf_op jit(solution)/shard_map/ppermute | solution.py:9
  53.5 17.3 %collective-permute-start.11 = (bf16[2,128,128]{2,1,0:T(8,128)(2,1)S(1)}, bf16[2,128,128]{2,1,0:T(8,128)(2,1)S(1)}, u32[]{:S(2)}, u32[]{:S(2)}) collective-permute-start(bf16[2,128,128]{2,1,0:T(8,128)(2,1)S(1)} %pad_maximum_fusion.9), channel_id=1, source_target_pairs={{0,8},{4,12},{8,16},{12,20},{16,24},{20,28},{24,32},{28,36},{32,40... | collective-permute-start | bytes 196616 | tf_op jit(solution)/shard_map/ppermute | solution.py:9
  75.3 16.0 %collective-permute-start.1 = (bf16[4,128,128]{2,1,0:T(8,128)(2,1)S(1)}, bf16[4,128,128]{2,1,0:T(8,128)(2,1)}, u32[]{:S(2)}, u32[]{:S(2)}) collective-permute-start(bf16[4,128,128]{2,1,0:T(8,128)(2,1)S(1)} %copy.100), channel_id=1, source_target_pairs={{0,16},{4,20},{8,24},{12,28},{16,32},{20,36},{24,40},{28,44},{32,4... | collective-permute-start | bytes 393224 | tf_op jit(solution)/shard_map/while/body/eval_jaxpr/ppermute | solution.py:9
  81.0 18.3 %collective-permute-start.2 = (f32[4,128,128]{2,1,0:T(8,128)S(1)}, f32[4,128,128]{2,1,0:T(8,128)S(1)}, u32[]{:S(2)}, u32[]{:S(2)}) collective-permute-start(f32[4,128,128]{2,1,0:T(8,128)S(1)} %maximum_add_fusion.6), channel_id=1, source_target_pairs={{0,16},{4,20},{8,24},{12,28},{16,32},{20,36},{24,40},{28,44},{32,4... | collective-permute-start | bytes 786440 | tf_op jit(solution)/shard_map/while/body/eval_jaxpr/ppermute | solution.py:9
  83.6 18.5 %collective-permute-start.3 = (f32[4,128,128]{2,1,0:T(8,128)}, f32[4,128,128]{2,1,0:T(8,128)S(1)}, u32[]{:S(2)}, u32[]{:S(2)}) collective-permute-start(f32[4,128,128]{2,1,0:T(8,128)} %maximum_add_fusion.7), channel_id=1, source_target_pairs={{0,16},{4,20},{8,24},{12,28},{16,32},{20,36},{24,40},{28,44},{32,4... | collective-permute-start | bytes 786440 | tf_op jit(solution)/shard_map/while/body/eval_jaxpr/ppermute | solution.py:9
  103.8 15.7 %collective-permute-start = (bf16[4,128,128]{2,1,0:T(8,128)(2,1)S(1)}, bf16[4,128,128]{2,1,0:T(8,128)(2,1)}, u32[]{:S(2)}, u32[]{:S(2)}) collective-permute-start(bf16[4,128,128]{2,1,0:T(8,128)(2,1)S(1)} %copy.99), channel_id=1, source_target_pairs={{0,16},{4,20},{8,24},{12,28},{16,32},{20,36},{24,40},{28,44},{32,4... | collective-permute-start | bytes 393224 | tf_op jit(solution)/shard_map/while/body/eval_jaxpr/ppermute | solution.py:9
  106.6 16.5 %collective-permute-start.1 = (bf16[4,128,128]{2,1,0:T(8,128)(2,1)S(1)}, bf16[4,128,128]{2,1,0:T(8,128)(2,1)}, u32[]{:S(2)}, u32[]{:S(2)}) collective-permute-start(bf16[4,128,128]{2,1,0:T(8,128)(2,1)S(1)} %copy.100), channel_id=1, source_target_pairs={{0,16},{4,20},{8,24},{12,28},{16,32},{20,36},{24,40},{28,44},{32,4... | collective-permute-start | bytes 393224 | tf_op jit(solution)/shard_map/while/body/eval_jaxpr/ppermute | solution.py:9
  112.3 18.3 %collective-permute-start.2 = (f32[4,128,128]{2,1,0:T(8,128)S(1)}, f32[4,128,128]{2,1,0:T(8,128)S(1)}, u32[]{:S(2)}, u32[]{:S(2)}) collective-permute-start(f32[4,128,128]{2,1,0:T(8,128)S(1)} %maximum_add_fusion.6), channel_id=1, source_target_pairs={{0,16},{4,20},{8,24},{12,28},{16,32},{20,36},{24,40},{28,44},{32,4... | collective-permute-start | bytes 786440 | tf_op jit(solution)/shard_map/while/body/eval_jaxpr/ppermute | solution.py:9
  114.9 18.5 %collective-permute-start.3 = (f32[4,128,128]{2,1,0:T(8,128)}, f32[4,128,128]{2,1,0:T(8,128)S(1)}, u32[]{:S(2)}, u32[]{:S(2)}) collective-permute-start(f32[4,128,128]{2,1,0:T(8,128)} %maximum_add_fusion.7), channel_id=1, source_target_pairs={{0,16},{4,20},{8,24},{12,28},{16,32},{20,36},{24,40},{28,44},{32,4... | collective-permute-start | bytes 786440 | tf_op jit(solution)/shard_map/while/body/eval_jaxpr/ppermute | solution.py:9
  135.1 15.7 %collective-permute-start = (bf16[4,128,128]{2,1,0:T(8,128)(2,1)S(1)}, bf16[4,128,128]{2,1,0:T(8,128)(2,1)}, u32[]{:S(2)}, u32[]{:S(2)}) collective-permute-start(bf16[4,128,128]{2,1,0:T(8,128)(2,1)S(1)} %copy.99), channel_id=1, source_target_pairs={{0,16},{4,20},{8,24},{12,28},{16,32},{20,36},{24,40},{28,44},{32,4... | collective-permute-start | bytes 393224 | tf_op jit(solution)/shard_map/while/body/eval_jaxpr/ppermute | solution.py:9
  137.9 16.5 %collective-permute-start.1 = (bf16[4,128,128]{2,1,0:T(8,128)(2,1)S(1)}, bf16[4,128,128]{2,1,0:T(8,128)(2,1)}, u32[]{:S(2)}, u32[]{:S(2)}) collective-permute-start(bf16[4,128,128]{2,1,0:T(8,128)(2,1)S(1)} %copy.100), channel_id=1, source_target_pairs={{0,16},{4,20},{8,24},{12,28},{16,32},{20,36},{24,40},{28,44},{32,4... | collective-permute-start | bytes 393224 | tf_op jit(solution)/shard_map/while/body/eval_jaxpr/ppermute | solution.py:9
  143.6 18.3 %collective-permute-start.2 = (f32[4,128,128]{2,1,0:T(8,128)S(1)}, f32[4,128,128]{2,1,0:T(8,128)S(1)}, u32[]{:S(2)}, u32[]{:S(2)}) collective-permute-start(f32[4,128,128]{2,1,0:T(8,128)S(1)} %maximum_add_fusion.6), channel_id=1, source_target_pairs={{0,16},{4,20},{8,24},{12,28},{16,32},{20,36},{24,40},{28,44},{32,4... | collective-permute-start | bytes 786440 | tf_op jit(solution)/shard_map/while/body/eval_jaxpr/ppermute | solution.py:9
  146.2 18.5 %collective-permute-start.3 = (f32[4,128,128]{2,1,0:T(8,128)}, f32[4,128,128]{2,1,0:T(8,128)S(1)}, u32[]{:S(2)}, u32[]{:S(2)}) collective-permute-start(f32[4,128,128]{2,1,0:T(8,128)} %maximum_add_fusion.7), channel_id=1, source_target_pairs={{0,16},{4,20},{8,24},{12,28},{16,32},{20,36},{24,40},{28,44},{32,4... | collective-permute-start | bytes 786440 | tf_op jit(solution)/shard_map/while/body/eval_jaxpr/ppermute | solution.py:9
  169.2 16.5 %collective-permute-start.1 = (bf16[4,128,128]{2,1,0:T(8,128)(2,1)S(1)}, bf16[4,128,128]{2,1,0:T(8,128)(2,1)}, u32[]{:S(2)}, u32[]{:S(2)}) collective-permute-start(bf16[4,128,128]{2,1,0:T(8,128)(2,1)S(1)} %copy.100), channel_id=1, source_target_pairs={{0,16},{4,20},{8,24},{12,28},{16,32},{20,36},{24,40},{28,44},{32,4... | collective-permute-start | bytes 393224 | tf_op jit(solution)/shard_map/while/body/eval_jaxpr/ppermute | solution.py:9
  174.9 18.3 %collective-permute-start.2 = (f32[4,128,128]{2,1,0:T(8,128)S(1)}, f32[4,128,128]{2,1,0:T(8,128)S(1)}, u32[]{:S(2)}, u32[]{:S(2)}) collective-permute-start(f32[4,128,128]{2,1,0:T(8,128)S(1)} %maximum_add_fusion.6), channel_id=1, source_target_pairs={{0,16},{4,20},{8,24},{12,28},{16,32},{20,36},{24,40},{28,44},{32,4... | collective-permute-start | bytes 786440 | tf_op jit(solution)/shard_map/while/body/eval_jaxpr/ppermute | solution.py:9
  177.5 18.5 %collective-permute-start.3 = (f32[4,128,128]{2,1,0:T(8,128)}, f32[4,128,128]{2,1,0:T(8,128)S(1)}, u32[]{:S(2)}, u32[]{:S(2)}) collective-permute-start(f32[4,128,128]{2,1,0:T(8,128)} %maximum_add_fusion.7), channel_id=1, source_target_pairs={{0,16},{4,20},{8,24},{12,28},{16,32},{20,36},{24,40},{28,44},{32,4... | collective-permute-start | bytes 786440 | tf_op jit(solution)/shard_map/while/body/eval_jaxpr/ppermute | solution.py:9
  200.5 16.5 %collective-permute-start.1 = (bf16[4,128,128]{2,1,0:T(8,128)(2,1)S(1)}, bf16[4,128,128]{2,1,0:T(8,128)(2,1)}, u32[]{:S(2)}, u32[]{:S(2)}) collective-permute-start(bf16[4,128,128]{2,1,0:T(8,128)(2,1)S(1)} %copy.100), channel_id=1, source_target_pairs={{0,16},{4,20},{8,24},{12,28},{16,32},{20,36},{24,40},{28,44},{32,4... | collective-permute-start | bytes 393224 | tf_op jit(solution)/shard_map/while/body/eval_jaxpr/ppermute | solution.py:9
  206.2 18.3 %collective-permute-start.2 = (f32[4,128,128]{2,1,0:T(8,128)S(1)}, f32[4,128,128]{2,1,0:T(8,128)S(1)}, u32[]{:S(2)}, u32[]{:S(2)}) collective-permute-start(f32[4,128,128]{2,1,0:T(8,128)S(1)} %maximum_add_fusion.6), channel_id=1, source_target_pairs={{0,16},{4,20},{8,24},{12,28},{16,32},{20,36},{24,40},{28,44},{32,4... | collective-permute-start | bytes 786440 | tf_op jit(solution)/shard_map/while/body/eval_jaxpr/ppermute | solution.py:9
  208.8 18.5 %collective-permute-start.3 = (f32[4,128,128]{2,1,0:T(8,128)}, f32[4,128,128]{2,1,0:T(8,128)S(1)}, u32[]{:S(2)}, u32[]{:S(2)}) collective-permute-start(f32[4,128,128]{2,1,0:T(8,128)} %maximum_add_fusion.7), channel_id=1, source_target_pairs={{0,16},{4,20},{8,24},{12,28},{16,32},{20,36},{24,40},{28,44},{32,4... | collective-permute-start | bytes 786440 | tf_op jit(solution)/shard_map/while/body/eval_jaxpr/ppermute | solution.py:9
  231.8 16.5 %collective-permute-start.1 = (bf16[4,128,128]{2,1,0:T(8,128)(2,1)S(1)}, bf16[4,128,128]{2,1,0:T(8,128)(2,1)}, u32[]{:S(2)}, u32[]{:S(2)}) collective-permute-start(bf16[4,128,128]{2,1,0:T(8,128)(2,1)S(1)} %copy.100), channel_id=1, source_target_pairs={{0,16},{4,20},{8,24},{12,28},{16,32},{20,36},{24,40},{28,44},{32,4... | collective-permute-start | bytes 393224 | tf_op jit(solution)/shard_map/while/body/eval_jaxpr/ppermute | solution.py:9
  237.5 18.3 %collective-permute-start.2 = (f32[4,128,128]{2,1,0:T(8,128)S(1)}, f32[4,128,128]{2,1,0:T(8,128)S(1)}, u32[]{:S(2)}, u32[]{:S(2)}) collective-permute-start(f32[4,128,128]{2,1,0:T(8,128)S(1)} %maximum_add_fusion.6), channel_id=1, source_target_pairs={{0,16},{4,20},{8,24},{12,28},{16,32},{20,36},{24,40},{28,44},{32,4... | collective-permute-start | bytes 786440 | tf_op jit(solution)/shard_map/while/body/eval_jaxpr/ppermute | solution.py:9
  240.1 18.5 %collective-permute-start.3 = (f32[4,128,128]{2,1,0:T(8,128)}, f32[4,128,128]{2,1,0:T(8,128)S(1)}, u32[]{:S(2)}, u32[]{:S(2)}) collective-permute-start(f32[4,128,128]{2,1,0:T(8,128)} %maximum_add_fusion.7), channel_id=1, source_target_pairs={{0,16},{4,20},{8,24},{12,28},{16,32},{20,36},{24,40},{28,44},{32,4... | collective-permute-start | bytes 786440 | tf_op jit(solution)/shard_map/while/body/eval_jaxpr/ppermute | solution.py:9
  263.1 16.5 %collective-permute-start.1 = (bf16[4,128,128]{2,1,0:T(8,128)(2,1)S(1)}, bf16[4,128,128]{2,1,0:T(8,128)(2,1)}, u32[]{:S(2)}, u32[]{:S(2)}) collective-permute-start(bf16[4,128,128]{2,1,0:T(8,128)(2,1)S(1)} %copy.100), channel_id=1, source_target_pairs={{0,16},{4,20},{8,24},{12,28},{16,32},{20,36},{24,40},{28,44},{32,4... | collective-permute-start | bytes 393224 | tf_op jit(solution)/shard_map/while/body/eval_jaxpr/ppermute | solution.py:9
  268.8 18.3 %collective-permute-start.2 = (f32[4,128,128]{2,1,0:T(8,128)S(1)}, f32[4,128,128]{2,1,0:T(8,128)S(1)}, u32[]{:S(2)}, u32[]{:S(2)}) collective-permute-start(f32[4,128,128]{2,1,0:T(8,128)S(1)} %maximum_add_fusion.6), channel_id=1, source_target_pairs={{0,16},{4,20},{8,24},{12,28},{16,32},{20,36},{24,40},{28,44},{32,4... | collective-permute-start | bytes 786440 | tf_op jit(solution)/shard_map/while/body/eval_jaxpr/ppermute | solution.py:9
  271.4 18.5 %collective-permute-start.3 = (f32[4,128,128]{2,1,0:T(8,128)}, f32[4,128,128]{2,1,0:T(8,128)S(1)}, u32[]{:S(2)}, u32[]{:S(2)}) collective-permute-start(f32[4,128,128]{2,1,0:T(8,128)} %maximum_add_fusion.7), channel_id=1, source_target_pairs={{0,16},{4,20},{8,24},{12,28},{16,32},{20,36},{24,40},{28,44},{32,4... | collective-permute-start | bytes 786440 | tf_op jit(solution)/shard_map/while/body/eval_jaxpr/ppermute | solution.py:9
  294.4 16.6 %collective-permute-start.1 = (bf16[4,128,128]{2,1,0:T(8,128)(2,1)S(1)}, bf16[4,128,128]{2,1,0:T(8,128)(2,1)}, u32[]{:S(2)}, u32[]{:S(2)}) collective-permute-start(bf16[4,128,128]{2,1,0:T(8,128)(2,1)S(1)} %copy.100), channel_id=1, source_target_pairs={{0,16},{4,20},{8,24},{12,28},{16,32},{20,36},{24,40},{28,44},{32,4... | collective-permute-start | bytes 393224 | tf_op jit(solution)/shard_map/while/body/eval_jaxpr/ppermute | solution.py:9
  300.1 18.4 %collective-permute-start.2 = (f32[4,128,128]{2,1,0:T(8,128)S(1)}, f32[4,128,128]{2,1,0:T(8,128)S(1)}, u32[]{:S(2)}, u32[]{:S(2)}) collective-permute-start(f32[4,128,128]{2,1,0:T(8,128)S(1)} %maximum_add_fusion.6), channel_id=1, source_target_pairs={{0,16},{4,20},{8,24},{12,28},{16,32},{20,36},{24,40},{28,44},{32,4... | collective-permute-start | bytes 786440 | tf_op jit(solution)/shard_map/while/body/eval_jaxpr/ppermute | solution.py:9
  302.7 18.6 %collective-permute-start.3 = (f32[4,128,128]{2,1,0:T(8,128)}, f32[4,128,128]{2,1,0:T(8,128)S(1)}, u32[]{:S(2)}, u32[]{:S(2)}) collective-permute-start(f32[4,128,128]{2,1,0:T(8,128)} %maximum_add_fusion.7), channel_id=1, source_target_pairs={{0,16},{4,20},{8,24},{12,28},{16,32},{20,36},{24,40},{28,44},{32,4... | collective-permute-start | bytes 786440 | tf_op jit(solution)/shard_map/while/body/eval_jaxpr/ppermute | solution.py:9
  324.2 21.3 %collective-permute-start.16 = (f32[2,128,128]{2,1,0:T(8,128)S(1)}, f32[2,128,128]{2,1,0:T(8,128)S(1)}, u32[]{:S(2)}, u32[]{:S(2)}) collective-permute-start(f32[2,128,128]{2,1,0:T(8,128)S(1)} %slice.236), channel_id=1, source_target_pairs={{0,504},{4,508},{8,0},{12,4},{16,8},{20,12},{24,16},{28,20},{32,24... | collective-permute-start | bytes 393224 | tf_op jit(solution)/shard_map/ppermute | solution.py:9
  (131 other events, 958.3 us)
